TPU v7x, 128 devices: a whole 4x4x4 slice. The times are simulated.
128 devices in a mesh: dp: 16 (over y, z), mp: 8 (over x, core).
Axes of the slice: x: 4, y: 4, z: 4, core: 2. Of those that a mesh axis runs over, the one named last changes fastest.
Arguments:
- grad_out: bfloat16 [16384, 6144], P(('dp', 'mp')), may hold values from -40 to 40
- context: bfloat16 [16384, 6144], P('dp', 'mp'), may hold values from -47 to 47
- weight: bfloat16 [6144, 6144], P(None, 'mp'), may hold values from -0.078125 to 0.078125
- master: float32 [6144, 6144], P('dp', 'mp'), may hold values from -0.6 to 0.6
- moment_q: bfloat16 [6144, 6144], P('dp', 'mp'), may hold values from -440 to 440
- second_moment: float32 [6144, 6144], P('dp', 'mp'), may hold values from 0.02 to 1
- moment_scale: float32 [], replicated, may hold values from 300 to 900
- scale_boost: float32 [], replicated, may hold values from 1.25 to 2
Outputs:
- input_grad: bfloat16 [16384, 6144], P('dp', 'mp')
- new_master: float32 [6144, 6144], P('dp', 'mp')
- new_moment_q: bfloat16 [6144, 6144], P('dp', 'mp')
- new_second: float32 [6144, 6144], P('dp', 'mp')
- new_scale: float32 [], replicated
- grad_scale: float32 [], replicated
- new_weight: bfloat16 [6144, 6144], P(None, 'mp')
All inputs are finite; a program needn't handle non-finite values. Where the computation divides by a largest or mean magnitude, that divisor is 1e-20 or more.
Results may differ from a plain program's by a relative error of at most 0.014.
Values may be sent and summed in bfloat16 or wider, within the bound.
No kernel may reach another device: no remote copies, remote signals or barrier semaphores. Data moves between devices by JAX's collectives and lax.ppermute only.
A program may use at most 128 MiB of HBM per device.

v0:
```python
import math
import jax
import jax.numpy as jnp
from jax import lax
from jax.sharding import PartitionSpec as P

D = 6144
HD = 6144
quant_top = 448.0
peak_eps = 1e-06
norm_eps = 1e-06
clip_rms = 0.5
beta_one = 0.9
beta_two = 0.95
bias_one = 1.0 - 0.9**10
bias_two = 1.0 - 0.95**10
adam_eps = 1e-08
rate_value = 0.01
decay_value = 0.1
contract_rows = (((0,), (0,)), ((), ()))


def input_product(full_grad, weight):
    return jnp.dot(full_grad, weight, preferred_element_type=jnp.float32).astype(jnp.bfloat16)


def weight_gradient(full_grad, context, scale_boost):
    held = lax.dot_general(full_grad, context, contract_rows, preferred_element_type=jnp.float32)
    local_peak = jnp.max(jnp.abs(held))
    peak = lax.pmax(local_peak, ("dp", "mp"))
    grad_scale = quant_top * scale_boost / (peak + peak_eps)
    scaled = held * grad_scale
    summed = lax.psum_scatter(
        jnp.clip(scaled, -quant_top, quant_top).astype(jnp.bfloat16),
        "dp",
        scatter_dimension=0,
        tiled=True,
    ).astype(jnp.float32)
    return (summed, grad_scale)


def local(grad_out, context, weight, master, moment_q, second_moment, moment_scale, scale_boost):
    full_grad = lax.all_gather(grad_out, "mp", axis=0, tiled=True)
    input_grad = input_product(full_grad, weight)
    summed, grad_scale = weight_gradient(full_grad, context, scale_boost)
    gradient = summed / grad_scale
    squares = lax.psum(jnp.sum(gradient * gradient), ("dp", "mp"))
    norm_value = jnp.sqrt(squares + norm_eps)
    clip_factor = clip_rms * math.sqrt(D * HD) / norm_value
    step_grad = clip_factor * gradient
    old_moment = moment_q.astype(jnp.float32) / moment_scale
    moment = beta_one * old_moment + (1.0 - beta_one) * step_grad
    new_second = beta_two * second_moment + (1.0 - beta_two) * step_grad * step_grad
    update = moment / bias_one / (jnp.sqrt(new_second / bias_two) + adam_eps) + decay_value * master
    new_master = master - rate_value * update
    moment_top = lax.pmax(jnp.max(jnp.abs(moment)), ("dp", "mp"))
    new_scale = quant_top / (moment_top + peak_eps)
    new_moment_q = (moment * new_scale).astype(jnp.bfloat16)
    new_weight = lax.all_gather(new_master.astype(jnp.bfloat16), "dp", axis=0, tiled=True)
    return (input_grad, new_master, new_moment_q, new_second, new_scale, grad_scale, new_weight)


def solution(mesh):
    return jax.shard_map(
        local,
        mesh=mesh,
        in_specs=(
            P(("dp", "mp"), None),
            P("dp", "mp"),
            P(None, "mp"),
            P("dp", "mp"),
            P("dp", "mp"),
            P("dp", "mp"),
            P(),
            P(),
        ),
        out_specs=(
            P("dp", "mp"),
            P("dp", "mp"),
            P("dp", "mp"),
            P("dp", "mp"),
            P(),
            P(),
            P(None, "mp"),
        ),
        check_vma=False,
    )
```

profile of v0, /device:TPU:1, one launch (start us, length us, event | category | flops | bytes accessed | tf_op | source)
XLA Modules:
  0.0 430.7 jit_solution(13931755045824228183)
XLA Ops:
  7.2 0.0 copy-start
  7.2 0.0 all-gather.3.cloned.1.call-start
  7.2 0.7 all-gather.3.cloned.1.call-update
  7.9 0.0 reduce-scatter.2.cloned.1.call-start
  8.6 72.1 %all-gather.3.cloned.1.call-done = bf16[1024,6144]{1,0:T(8,128)(2,1)} async-done(((bf16[128,6144]{1,0:T(8,128)(2,1)}), bf16[1024,6144]{1,0:T(8,128)(2,1)}) %all-gather.3.cloned.1.call-update) | async-done | bytes 12582928 | tf_op jit(solution)/shard_map/all_gather | solution.py:43
  80.7 0.0 copy-done
  80.7 17.7 %abs_reduce_fusion = (f32[]{:T(128)}, f32[6144,768]{1,0:T(8,128)}) fusion(bf16[1024,6144]{1,0:T(8,128)(2,1)} %all-gather.3.cloned.1.call-done, bf16[1024,768]{1,0:T(8,128)(2,1)S(1)} %copy-done), kind=kOutput, calls=%fused_computation.1 | convolution fusion | flops 9673113600 | bytes 33030148 | tf_op jit(solution)/shard_map/dot_general | solution.py:28
  98.3 64.9 %pmax.14 = f32[]{:T(128)} all-reduce(f32[]{:T(128)} %get-tuple-element.11), channel_id=1, replica_groups=mesh['dp'=16,'mp'=8] {'dp','mp'}, use_global_device_ids=true, to_apply=%region_1.0 | all-reduce | flops 1 | bytes 8 | tf_op jit(solution)/shard_map/pmax | solution.py:30
  164.0 11.6 %clamp_convert_fusion = bf16[6144,768]{1,0:T(8,128)(2,1)} fusion(f32[6144,768]{1,0:T(8,128)} %get-tuple-element.12, f32[]{:T(128)} %div.38), kind=kLoop, calls=%fused_computation | loop fusion | flops 14155776 | bytes 28311556 | tf_op jit(solution)/shard_map/convert_element_type | solution.py:34
  175.5 0.0 reduce-scatter.2.cloned.1.call-update
  175.5 0.0 all-gather.5.cloned.1.call-start
  175.6 83.8 %reduce-scatter.2.cloned.1.call-done = bf16[384,768]{1,0:T(8,128)(2,1)} async-done(((bf16[6144,768]{1,0:T(8,128)(2,1)}), bf16[384,768]{1,0:T(8,128)(2,1)}) %reduce-scatter.2.cloned.1.call-update) | async-done | bytes 589840 | tf_op jit(solution)/shard_map/reduce_scatter | solution.py:33
  259.4 2.0 multiply_reduce_fusion
  262.0 65.6 %psum.7 = f32[]{:T(128)} all-reduce(f32[]{:T(128)} %multiply_reduce_fusion), channel_id=1, replica_groups=mesh['dp'=16,'mp'=8] {'dp','mp'}, use_global_device_ids=true, to_apply=%region_4.5 | all-reduce | flops 1 | bytes 8 | tf_op jit(solution)/shard_map/psum | solution.py:47
  328.3 0.0 copy-done.2
  328.3 0.0 copy-done.3
  328.3 4.1 fusion.1
  332.4 0.0 all-gather.5.cloned.1.call-update
  332.5 0.7 abs_reduce_fusion.1
  333.1 15.6 %convolution_convert_fusion = bf16[1024,768]{1,0:T(8,128)(2,1)} fusion(bf16[1024,6144]{1,0:T(8,128)(2,1)} %all-gather.3.cloned.1.call-done, bf16[6144,768]{1,0:T(8,128)(2,1)} %param.10), kind=kOutput, calls=%fused_computation.3 | convolution fusion | flops 9664462848 | bytes 23592960 | tf_op jit(solution)/shard_map/dot_general | solution.py:24
  348.8 63.4 %pmax.15 = f32[]{:T(128)} all-reduce(f32[]{:T(128)} %abs_reduce_fusion.1), channel_id=1, replica_groups=mesh['dp'=16,'mp'=8] {'dp','mp'}, use_global_device_ids=true, to_apply=%region_6.7 | all-reduce | flops 1 | bytes 8 | tf_op jit(solution)/shard_map/pmax | solution.py:56
  412.9 0.9 multiply_convert_fusion
  413.8 8.1 %copy.18 = bf16[6144,768]{1,0:T(8,128)(2,1)} copy(bf16[6144,768]{1,0:T(8,128)(2,1)} %all-gather.5.cloned.1.call-done) | data formatting | bytes 18874368
  421.9 0.0 copy-done.1
  (4 shorter events, 0.0 us)
Async XLA Ops:
  7.2 73.5 %copy-start = (bf16[1024,768]{1,0:T(8,128)(2,1)S(1)}, bf16[1024,768]{1,0:T(8,128)(2,1)}, u32[]{:S(2)}) copy-start(bf16[1024,768]{1,0:T(8,128)(2,1)} %param.9) | copy-start | bytes 4718596
  7.2 73.5 %all-gather.3.cloned.1.call-start = ((), (), s32[]{:S(2)}) async-start(), calls=%async_computation.1 | async-start | bytes 14155776 | tf_op jit(solution)/shard_map/all_gather | solution.py:43
  7.9 251.5 %reduce-scatter.2.cloned.1.call-start = ((), (), s32[]{:S(2)}) async-start(), calls=%async_computation.2 | async-start | bytes 10027008 | tf_op jit(solution)/shard_map/reduce_scatter | solution.py:33
  175.5 152.8 %copy-start.2 = (f32[384,768]{1,0:T(8,128)S(1)}, f32[384,768]{1,0:T(8,128)}, u32[]{:S(2)}) copy-start(f32[384,768]{1,0:T(8,128)} %param.11) | copy-start | bytes 3538948
  175.5 152.8 %copy-start.3 = (bf16[384,768]{1,0:T(8,128)(2,1)S(1)}, bf16[384,768]{1,0:T(8,128)(2,1)}, u32[]{:S(2)}) copy-start(bf16[384,768]{1,0:T(8,128)(2,1)} %param.12) | copy-start | bytes 1769476
  175.5 238.2 %all-gather.5.cloned.1.call-start = ((), (), s32[]{:S(2)}) async-start(), calls=%async_computation.3 | async-start | bytes 10027008 | tf_op jit(solution)/shard_map/all_gather | solution.py:59
  413.8 8.2 %copy-start.1 = (bf16[1024,768]{1,0:T(8,128)(2,1)S(1)}, bf16[1024,768]{1,0:T(8,128)(2,1)}, u32[]{:S(2)}) copy-start(bf16[1024,768]{1,0:T(8,128)(2,1)} %param.9) | copy-start | bytes 4718596
Sparse Core Ops, SparseCore 0:
  9.7 70.9 all-gather.2
  175.7 83.6 reduce-scatter.1
  332.6 72.7 all-gather.4
where the time goes:
time: 431 us
  blocking collectives  194 us (45%)
  waiting for transfers between devices  157 us (36%)
  matrix products  33.3 us (8%)
  between operations  19.4 us (5%)
  other arithmetic  19.2 us (4%)
  local copies, waits for them, and re-layouts  8.17 us (2%)
    reduce_scatter x1, waiting for transfers between devices, weight_gradient(): lax.psum_scatter(jnp.clip(scaled, -quant_top, quant_top).astype(jnp.bfloa...  83.8 us
    all_gather x1, waiting for transfers between devices, local(): full_grad = lax.all_gather(grad_out, 'mp', axis=0, tiled=True)  72.1 us
    psum x1, blocking collectives, local(): squares = lax.psum(jnp.sum(gradient * gradient), ('dp', 'mp'))  65.6 us
    pmax x1, blocking collectives, weight_gradient(): peak = lax.pmax(local_peak, ('dp', 'mp'))  64.9 us
    pmax x1, blocking collectives, local(): moment_top = lax.pmax(jnp.max(jnp.abs(moment)), ('dp', 'mp'))  63.4 us
    dot_general x1, matrix products, weight_gradient(): lax.dot_general(full_grad, context, contract_rows, preferred_element_type...  17.7 us
    dot_general x1, matrix products, input_product(): jnp.dot(full_grad, weight, preferred_element_type=jnp.float32)  15.6 us
    convert_element_type x1, other arithmetic, weight_gradient(): jnp.clip(scaled, -quant_top, quant_top).astype(jnp.bfloat16)  11.6 us
  transfers between devices with their start and end apart: 3, of which 2 were waited for; matrix products, arithmetic and copies ran while one was open for 4% of the time, Pallas kernels for 0%

commit v1 on v0

--- a/solution.py
+++ b/solution.py
@@ -40,7 +40,8 @@
 
 
 def local(grad_out, context, weight, master, moment_q, second_moment, moment_scale, scale_boost):
-    full_grad = lax.all_gather(grad_out, "mp", axis=0, tiled=True)
+    repeated = jnp.stack([grad_out] * lax.axis_size("mp"))
+    full_grad = jnp.concatenate(lax.all_to_all(repeated, "mp", 0, 0), axis=0)
     input_grad = input_product(full_grad, weight)
     summed, grad_scale = weight_gradient(full_grad, context, scale_boost)
     gradient = summed / grad_scale

time: 431 us -> 513 us (1.19)
  waiting for transfers between devices: 157 us -> 222 us
  local copies, waits for them, and re-layouts: 8.17 us -> 15.8 us
  starting transfers between devices: 0.12 us -> 6.69 us
    all_to_all x0 -> x1, waiting for transfers between devices: none -> 138 us  [local(): full_grad = jnp.concatenate(lax.all_to_all(repeated, 'mp', 0, 0), axis=0)]
    all_gather x1 -> x0, waiting for transfers between devices: 72.1 us -> none  [local(): full_grad = lax.all_gather(grad_out, 'mp', axis=0, tiled=True)]
    another operation x0 -> x1, local copies, waits for them, and re-layouts: none -> 7.67 us  [local(): repeated = jnp.stack([grad_out] * lax.axis_size('mp'))]
    all_to_all x0 -> x1, starting transfers between devices: none -> 6.64 us  [local(): full_grad = jnp.concatenate(lax.all_to_all(repeated, 'mp', 0, 0), axis=0)]
  transfers between devices with their start and end apart: 3 -> 3, of which waited for: 2 -> 2; matrix products, arithmetic and copies ran while one was open for 4% -> 3% of each run, Pallas kernels for 0% -> 0%
where the time goes in v1:
time: 513 us; the launch traced here: 512 us
  waiting for transfers between devices  222 us (43%)
  blocking collectives  195 us (38%)
  matrix products  33.3 us (6%)
  between operations  19.7 us (4%)
  other arithmetic  19.2 us (4%)
  local copies, waits for them, and re-layouts  15.8 us (3%)
  starting transfers between devices  6.69 us (1%)
    all_to_all x1, waiting for transfers between devices, local(): full_grad = jnp.concatenate(lax.all_to_all(repeated, 'mp', 0, 0), axis=0)  138 us
    reduce_scatter x1, waiting for transfers between devices, weight_gradient(): lax.psum_scatter(jnp.clip(scaled, -quant_top, quant_top).astype(jnp.bfloa...  83.8 us
    pmax x1, blocking collectives, weight_gradient(): peak = lax.pmax(local_peak, ('dp', 'mp'))  66.5 us
    psum x1, blocking collectives, local(): squares = lax.psum(jnp.sum(gradient * gradient), ('dp', 'mp'))  65.4 us
    pmax x1, blocking collectives, local(): moment_top = lax.pmax(jnp.max(jnp.abs(moment)), ('dp', 'mp'))  63.5 us
    dot_general x1, matrix products, weight_gradient(): lax.dot_general(full_grad, context, contract_rows, preferred_element_type...  17.7 us
    dot_general x1, matrix products, input_product(): jnp.dot(full_grad, weight, preferred_element_type=jnp.float32)  15.6 us
    convert_element_type x1, other arithmetic, weight_gradient(): jnp.clip(scaled, -quant_top, quant_top).astype(jnp.bfloat16)  11.6 us
  transfers between devices with their start and end apart: 3, of which 2 were waited for; matrix products, arithmetic and copies ran while one was open for 3% of the time, Pallas kernels for 0%

profile of v1, /device:TPU:1, one launch (start us, length us, event | category | flops | bytes accessed | tf_op | source)
XLA Modules:
  0.0 512.2 jit_solution(12556564231941878470)
XLA Ops:
  7.2 0.0 copy-start
  7.2 7.7 %stack.2 = bf16[8,128,6144]{2,1,0:T(8,128)(2,1)} broadcast(bf16[128,6144]{1,0:T(8,128)(2,1)} %param.8), dimensions={1,2} | broadcast | bytes 14155776 | tf_op jit(solution)/shard_map/stack | solution.py:43
  14.8 6.6 %all-to-all-start = ((bf16[8,128,6144]{2,1,0:T(8,128)(2,1)}), bf16[8,128,6144]{2,1,0:T(8,128)(2,1)}, u32[]{:S(2)}, u32[]{:S(2)}) async-start(bf16[8,128,6144]{2,1,0:T(8,128)(2,1)} %stack.2), calls=%async_computation | async-start | bytes 25165824 | tf_op jit(solution)/shard_map/all_to_all | solution.py:44
  21.5 0.0 reduce-scatter.2.cloned.1.call-start
  22.1 138.2 %all-to-all-done = bf16[8,128,6144]{2,1,0:T(8,128)(2,1)} async-done(((bf16[8,128,6144]{2,1,0:T(8,128)(2,1)}), bf16[8,128,6144]{2,1,0:T(8,128)(2,1)}, u32[]{:S(2)}, u32[]{:S(2)}) %all-to-all-start) | async-done | bytes 12582944 | tf_op jit(solution)/shard_map/all_to_all | solution.py:44
  160.3 0.0 copy-done
  160.3 17.7 %abs_reduce_fusion = (f32[]{:T(128)}, f32[6144,768]{1,0:T(8,128)}) fusion(bf16[1024,6144]{1,0:T(8,128)(2,1)} %bitcast, bf16[1024,768]{1,0:T(8,128)(2,1)S(1)} %copy-done), kind=kOutput, calls=%fused_computation.1 | convolution fusion | flops 9673113600 | bytes 33030148 | tf_op jit(solution)/shard_map/dot_general | solution.py:28
  178.0 66.5 %pmax.14 = f32[]{:T(128)} all-reduce(f32[]{:T(128)} %get-tuple-element.11), channel_id=1, replica_groups=mesh['dp'=16,'mp'=8] {'dp','mp'}, use_global_device_ids=true, to_apply=%region_1.0 | all-reduce | flops 1 | bytes 8 | tf_op jit(solution)/shard_map/pmax | solution.py:30
  245.2 11.6 %clamp_convert_fusion = bf16[6144,768]{1,0:T(8,128)(2,1)} fusion(f32[6144,768]{1,0:T(8,128)} %get-tuple-element.12, f32[]{:T(128)} %div.38), kind=kLoop, calls=%fused_computation | loop fusion | flops 14155776 | bytes 28311556 | tf_op jit(solution)/shard_map/convert_element_type | solution.py:34
  256.7 0.0 reduce-scatter.2.cloned.1.call-update
  256.8 0.0 all-gather.2.cloned.1.call-start
  256.8 83.8 %reduce-scatter.2.cloned.1.call-done = bf16[384,768]{1,0:T(8,128)(2,1)} async-done(((bf16[6144,768]{1,0:T(8,128)(2,1)}), bf16[384,768]{1,0:T(8,128)(2,1)}) %reduce-scatter.2.cloned.1.call-update) | async-done | bytes 589840 | tf_op jit(solution)/shard_map/reduce_scatter | solution.py:33
  340.6 2.0 multiply_reduce_fusion
  343.2 65.4 %psum.7 = f32[]{:T(128)} all-reduce(f32[]{:T(128)} %multiply_reduce_fusion), channel_id=1, replica_groups=mesh['dp'=16,'mp'=8] {'dp','mp'}, use_global_device_ids=true, to_apply=%region_4.5 | all-reduce | flops 1 | bytes 8 | tf_op jit(solution)/shard_map/psum | solution.py:48
  409.3 0.0 copy-done.2
  409.4 0.0 copy-done.3
  409.4 4.1 fusion.1
  413.5 0.0 all-gather.2.cloned.1.call-update
  413.5 0.7 abs_reduce_fusion.1
  414.2 15.6 %convolution_convert_fusion = bf16[1024,768]{1,0:T(8,128)(2,1)} fusion(bf16[1024,6144]{1,0:T(8,128)(2,1)} %bitcast, bf16[6144,768]{1,0:T(8,128)(2,1)} %param.10), kind=kOutput, calls=%fused_computation.3 | convolution fusion | flops 9664462848 | bytes 23592960 | tf_op jit(solution)/shard_map/dot_general | solution.py:24
  429.8 63.5 %pmax.15 = f32[]{:T(128)} all-reduce(f32[]{:T(128)} %abs_reduce_fusion.1), channel_id=1, replica_groups=mesh['dp'=16,'mp'=8] {'dp','mp'}, use_global_device_ids=true, to_apply=%region_6.7 | all-reduce | flops 1 | bytes 8 | tf_op jit(solution)/shard_map/pmax | solution.py:57
  494.0 0.9 multiply_convert_fusion
  494.9 8.1 %copy.18 = bf16[6144,768]{1,0:T(8,128)(2,1)} copy(bf16[6144,768]{1,0:T(8,128)(2,1)} %all-gather.2.cloned.1.call-done) | data formatting | bytes 18874368
  503.1 0.0 copy-done.1
  (4 shorter events, 0.0 us)
Async XLA Ops:
  7.2 153.1 %copy-start = (bf16[1024,768]{1,0:T(8,128)(2,1)S(1)}, bf16[1024,768]{1,0:T(8,128)(2,1)}, u32[]{:S(2)}) copy-start(bf16[1024,768]{1,0:T(8,128)(2,1)} %param.9) | copy-start | bytes 4718596
  14.8 145.5 %all-to-all-start = ((bf16[8,128,6144]{2,1,0:T(8,128)(2,1)}), bf16[8,128,6144]{2,1,0:T(8,128)(2,1)}, u32[]{:S(2)}, u32[]{:S(2)}) async-start(bf16[8,128,6144]{2,1,0:T(8,128)(2,1)} %stack.2), calls=%async_computation | async-start | bytes 25165824 | tf_op jit(solution)/shard_map/all_to_all | solution.py:44
  21.5 319.1 %reduce-scatter.2.cloned.1.call-start = ((), (), s32[]{:S(2)}) async-start(), calls=%async_computation.2 | async-start | bytes 10027008 | tf_op jit(solution)/shard_map/reduce_scatter | solution.py:33
  256.7 152.6 %copy-start.2 = (f32[384,768]{1,0:T(8,128)S(1)}, f32[384,768]{1,0:T(8,128)}, u32[]{:S(2)}) copy-start(f32[384,768]{1,0:T(8,128)} %param.11) | copy-start | bytes 3538948
  256.7 152.6 %copy-start.3 = (bf16[384,768]{1,0:T(8,128)(2,1)S(1)}, bf16[384,768]{1,0:T(8,128)(2,1)}, u32[]{:S(2)}) copy-start(bf16[384,768]{1,0:T(8,128)(2,1)} %param.12) | copy-start | bytes 1769476
  256.8 238.2 %all-gather.2.cloned.1.call-start = ((), (), s32[]{:S(2)}) async-start(), calls=%async_computation.3 | async-start | bytes 10027008 | tf_op jit(solution)/shard_map/all_gather | solution.py:60
  494.9 8.2 %copy-start.1 = (bf16[1024,768]{1,0:T(8,128)(2,1)S(1)}, bf16[1024,768]{1,0:T(8,128)(2,1)}, u32[]{:S(2)}) copy-start(bf16[1024,768]{1,0:T(8,128)(2,1)} %param.9) | copy-start | bytes 4718596
Sparse Core Ops, SparseCore 0:
  256.9 83.6 reduce-scatter.1
  413.6 72.8 all-gather.1
